TPU v7x, 128 devices: a whole 4x4x4 slice. The times are simulated.
128 devices in a mesh: dp: 16 (over y_lo, x, core), tensor: 8 (over y_hi, z).
Axes of the slice: x: 4, y: 4 (y_hi: 2, y_lo: 2; y = y_hi * 2 + y_lo), z: 4, core: 2. Of those that a mesh axis runs over, the one named last changes fastest.
Arguments:
- tokens: bfloat16 [12288, 2048], P('dp'), may hold values from -6 to 6
- cotangent: bfloat16 [12288, 2048], P('dp'), may hold values from -6 to 6
- segments: int32 [12288], replicated, may hold values from 0 to 15, never falling along the last dimension, each value on 1 to 1537 neighbouring positions
- attn_norm_gain: float32 [2048], P('dp'), may hold values from 0.5 to 1.5
- attn_norm_bias: float32 [2048], P('dp'), may hold values from -1.25 to 1.25
- query_weight: float32 [2048, 2048], P('dp', 'tensor'), may hold values from -0.125 to 0.125
- query_bias: float32 [16, 128], P('tensor', 'dp'), may hold values from -1.25 to 1.25
- kv_weight: float32 [2048, 256], P('dp'), may hold values from -0.125 to 0.125
- value_bias: float32 [128], P('dp'), may hold values from -1.25 to 1.25
- out_weight: float32 [2048, 2048], P('tensor', 'dp'), may hold values from -0.5 to 0.5
- out_bias: float32 [2048], P('dp'), may hold values from -1.25 to 1.25
- mlp_norm_gain: float32 [2048], P('dp'), may hold values from 0.5 to 1.5
- mlp_norm_bias: float32 [2048], P('dp'), may hold values from -1.25 to 1.25
- up_weight: float32 [2048, 8192], P('dp', 'tensor'), may hold values from -0.125 to 0.125
- up_bias: float32 [64, 128], P('tensor', 'dp'), may hold values from -1.25 to 1.25
- down_weight: float32 [8192, 2048], P('tensor', 'dp'), may hold values from -0.0625 to 0.0625
- down_bias: float32 [2048], P('dp'), may hold values from -1.25 to 1.25
Outputs:
- output: bfloat16 [12288, 2048], P('dp')
- input_grad: float32 [12288, 2048], P('dp')
- attn_norm_gain_grad: float32 [2048], P('dp')
- attn_norm_bias_grad: float32 [2048], P('dp')
- query_weight_grad: float32 [2048, 2048], P('dp', 'tensor')
- query_bias_grad: float32 [16, 128], P('tensor', 'dp')
- kv_weight_grad: float32 [2048, 256], P('dp')
- value_bias_grad: float32 [128], P('dp')
- out_weight_grad: float32 [2048, 2048], P('tensor', 'dp')
- out_bias_grad: float32 [2048], P('dp')
- mlp_norm_gain_grad: float32 [2048], P('dp')
- mlp_norm_bias_grad: float32 [2048], P('dp')
- up_weight_grad: float32 [2048, 8192], P('dp', 'tensor')
- up_bias_grad: float32 [64, 128], P('tensor', 'dp')
- down_weight_grad: float32 [8192, 2048], P('tensor', 'dp')
- down_bias_grad: float32 [2048], P('dp')
Inputs may be any that keep to these rules, and one draw needn't show every extreme that they name: `segments`: segment numbers never fall along the stream; every document spans 1 to 1537 consecutive tokens, and some document spans exactly 1537.
All inputs are finite; a program needn't handle non-finite values.
Results may differ from a plain program's by a relative error of at most 0.03.
Values may be sent and summed in bfloat16 or wider, within the bound.
A program may use at most 192 MiB of HBM per device.

v0:
```python
import math

import jax
import jax.numpy as jnp
from jax import lax
from jax.sharding import PartitionSpec as P

HD = 128
DOC_MOST = 2000


EPS = 1e-05
NEG = -1e30


def from_behind(value, axis, steps):
    count = lax.axis_size(axis)
    initial, last = (max(0, -steps), min(count, count - steps))
    return lax.ppermute(value, axis, [(source, source + steps) for source in range(initial, last)])


def norm_rows(values, gain, shift):
    center = values - jnp.mean(values, axis=-1, keepdims=True)
    spread = jnp.mean(center * center, axis=-1, keepdims=True)
    return center * lax.rsqrt(spread + EPS) * gain + shift


def gelu_tanh(upward):
    inner = 0.7978845608028654 * (upward + 0.044715 * upward * upward * upward)
    return 0.5 * upward * (1.0 + jnp.tanh(inner))


def matmul(left, right):
    return jnp.dot(left, right, preferred_element_type=jnp.float32)


def contract_rows(left, right):
    return lax.dot_general(
        left, right, (((0,), (0,)), ((), ())), preferred_element_type=jnp.float32
    )


def contract_cols(left, right):
    return lax.dot_general(
        left, right, (((1,), (1,)), ((), ())), preferred_element_type=jnp.float32
    )


def heads_to_rows(matrix, local_heads, tok_rows):
    return (
        matrix.reshape(tok_rows, local_heads, HD)
        .transpose(1, 0, 2)
        .reshape(local_heads * tok_rows, HD)
    )


def rows_to_heads(matrix, local_heads, tok_rows):
    return (
        matrix.reshape(local_heads, tok_rows, HD)
        .transpose(1, 0, 2)
        .reshape(tok_rows, local_heads * HD)
    )


def body(
    tokens,
    cotangent,
    segments,
    attn_norm_gain,
    attn_norm_bias,
    query_weight,
    query_bias,
    kv_weight,
    value_bias,
    out_weight,
    out_bias,
    mlp_norm_gain,
    mlp_norm_bias,
    up_weight,
    up_bias,
    down_weight,
    down_bias,
):
    dp_size = lax.axis_size("dp")
    tok_rows = tokens.shape[0]
    local_heads = query_bias.shape[0]
    reach = min((DOC_MOST - 1) // tok_rows, dp_size // 2)
    window = (reach + 1) * tok_rows
    block_index = lax.axis_index("dp")
    scale = 1.0 / math.sqrt(HD)
    bf16 = jnp.bfloat16
    f32 = jnp.float32
    gathered = (
        lax.all_gather(attn_norm_gain.astype(bf16), "dp", axis=0, tiled=True),
        lax.all_gather(attn_norm_bias.astype(bf16), "dp", axis=0, tiled=True),
        lax.all_gather(query_weight.astype(bf16), "dp", axis=0, tiled=True),
        lax.all_gather(query_bias.astype(bf16), "dp", axis=1, tiled=True),
        lax.all_gather(kv_weight.astype(bf16), "dp", axis=0, tiled=True),
        lax.all_gather(value_bias.astype(bf16), "dp", axis=0, tiled=True),
        lax.all_gather(out_weight.astype(bf16), "dp", axis=1, tiled=True),
        lax.all_gather(out_bias.astype(bf16), "dp", axis=0, tiled=True),
        lax.all_gather(mlp_norm_gain.astype(bf16), "dp", axis=0, tiled=True),
        lax.all_gather(mlp_norm_bias.astype(bf16), "dp", axis=0, tiled=True),
        lax.all_gather(up_weight.astype(bf16), "dp", axis=0, tiled=True),
        lax.all_gather(up_bias.astype(bf16), "dp", axis=1, tiled=True),
        lax.all_gather(down_weight.astype(bf16), "dp", axis=1, tiled=True),
        lax.all_gather(down_bias.astype(bf16), "dp", axis=0, tiled=True),
    )
    gain_one = gathered[0].astype(f32)
    shift_one = gathered[1].astype(f32)
    query_w = gathered[2]
    query_b = gathered[3].reshape(-1).astype(f32)
    kv_w = gathered[4]
    value_b = gathered[5].astype(f32)
    out_w = gathered[6]
    out_b = gathered[7].astype(f32)
    gain_two = gathered[8].astype(f32)
    shift_two = gathered[9].astype(f32)
    up_w = gathered[10]
    up_b = gathered[11].reshape(-1).astype(f32)
    down_w = gathered[12]
    down_b = gathered[13].astype(f32)
    inputs = tokens.astype(f32)
    normed_one, norm_one_back = jax.vjp(norm_rows, inputs, gain_one, shift_one)
    normed_one = normed_one.astype(bf16)
    query = (matmul(normed_one, query_w) + query_b).astype(bf16)
    value_shift = jnp.concatenate([jnp.zeros((HD,), f32), value_b])
    keyval = (matmul(normed_one, kv_w) + value_shift).astype(bf16)
    pieces = []
    for offset in range(reach, 0, -1):
        pieces.append(from_behind(keyval, "dp", offset))
    window_kv = jnp.concatenate(pieces + [keyval], 0)
    window_keys = window_kv[:, :HD]
    window_values = window_kv[:, HD:]
    seg_padded = jnp.concatenate([jnp.full((reach * tok_rows,), -1, jnp.int32), segments])
    key_seg = lax.dynamic_slice_in_dim(seg_padded, block_index * tok_rows, window)
    query_seg = lax.dynamic_slice_in_dim(segments, block_index * tok_rows, tok_rows)
    key_place = jnp.arange(window, dtype=jnp.int32)
    query_place = reach * tok_rows + jnp.arange(tok_rows, dtype=jnp.int32)
    allowed = (query_seg[:, None] == key_seg[None, :]) & (
        key_place[None, :] <= query_place[:, None]
    )
    allowed = jnp.tile(allowed, (local_heads, 1))
    query_rows = heads_to_rows(query, local_heads, tok_rows)
    scores = jnp.where(allowed, contract_cols(query_rows, window_keys) * scale, NEG)
    top = jnp.max(scores, axis=-1, keepdims=True)
    log_total = top + jnp.log(jnp.sum(jnp.exp(scores - top), axis=-1, keepdims=True))
    probs = jnp.exp(scores - log_total).astype(bf16)
    attended = rows_to_heads(matmul(probs, window_values), local_heads, tok_rows).astype(bf16)
    middle = inputs + lax.psum(matmul(attended, out_w), "tensor") + out_b
    normed_two, norm_two_back = jax.vjp(norm_rows, middle, gain_two, shift_two)
    normed_two = normed_two.astype(bf16)
    hidden, gelu_back = jax.vjp(gelu_tanh, matmul(normed_two, up_w) + up_b)
    hidden = hidden.astype(bf16)
    output = (
        middle
        + lax.psum(matmul(hidden, down_w).astype(jnp.bfloat16), "tensor").astype(jnp.float32)
        + down_b
    ).astype(bf16)
    down_bias_grad = jnp.sum(cotangent.astype(f32), axis=0)
    down_weight_grad = contract_rows(hidden, cotangent)
    grad_hidden = contract_cols(cotangent, down_w)
    grad_up = gelu_back(grad_hidden)[0].astype(bf16)
    up_bias_grad = jnp.sum(grad_up.astype(f32), axis=0).reshape(-1, HD)
    up_weight_grad = contract_rows(normed_two, grad_up)
    grad_norm_two = lax.psum(contract_cols(grad_up, up_w), "tensor")
    grad_middle, mlp_gain_grad, mlp_shift_grad = norm_two_back(grad_norm_two)
    grad_middle = grad_middle + cotangent.astype(f32)
    grad_attn = grad_middle.astype(bf16)
    out_bias_grad = jnp.sum(grad_attn.astype(f32), axis=0)
    out_weight_grad = contract_rows(attended, grad_attn)
    grad_attended = contract_cols(grad_attn, out_w).astype(bf16)
    grad_rows = heads_to_rows(grad_attended, local_heads, tok_rows)
    scores_again = jnp.where(allowed, contract_cols(query_rows, window_keys) * scale, NEG)
    probs_again = jnp.exp(scores_again - log_total)
    grad_probs = contract_cols(grad_rows, window_values)
    delta = jnp.sum(probs_again * grad_probs, axis=-1, keepdims=True)
    grad_scores = (probs_again * (grad_probs - delta)).astype(bf16)
    grad_query = rows_to_heads(
        matmul(grad_scores, window_keys) * scale, local_heads, tok_rows
    ).astype(bf16)
    grad_keys = contract_rows(grad_scores, query_rows) * scale
    grad_values = contract_rows(probs_again.astype(bf16), grad_rows)
    grad_window = jnp.concatenate([grad_keys, grad_values], 1)
    own_kv_grad = grad_window[reach * tok_rows :]
    for offset in range(1, reach + 1):
        piece = grad_window[(reach - offset) * tok_rows : (reach - offset + 1) * tok_rows]
        own_kv_grad = own_kv_grad + from_behind(piece.astype(jnp.bfloat16), "dp", -offset).astype(
            piece.dtype
        )
    query_part = contract_cols(grad_query, query_w)
    grad_norm_query, kv_grad_total = (
        lax.psum(query_part.astype(jnp.bfloat16), "tensor").astype(jnp.float32),
        lax.psum(own_kv_grad.astype(jnp.bfloat16), "tensor").astype(jnp.float32),
    )
    kv_grad = kv_grad_total.astype(bf16)
    value_bias_grad = jnp.sum(kv_grad[:, HD:].astype(f32), axis=0)
    kv_weight_grad = contract_rows(normed_one, kv_grad)
    query_bias_grad = jnp.sum(grad_query.astype(f32), axis=0).reshape(local_heads, HD)
    query_weight_grad = contract_rows(normed_one, grad_query)
    grad_norm_one = grad_norm_query + contract_cols(kv_grad, kv_w)
    grad_inputs, attn_gain_grad, attn_shift_grad = norm_one_back(grad_norm_one)
    input_grad = grad_middle + grad_inputs
    summed = tuple(
        (
            lax.psum_scatter(
                attn_gain_grad.astype(jnp.bfloat16), "dp", scatter_dimension=0, tiled=True
            ).astype(jnp.float32),
            lax.psum_scatter(
                attn_shift_grad.astype(jnp.bfloat16), "dp", scatter_dimension=0, tiled=True
            ).astype(jnp.float32),
            lax.psum_scatter(
                query_weight_grad.astype(jnp.bfloat16), "dp", scatter_dimension=0, tiled=True
            ).astype(jnp.float32),
            lax.psum_scatter(
                query_bias_grad.astype(jnp.bfloat16), "dp", scatter_dimension=1, tiled=True
            ).astype(jnp.float32),
            lax.psum_scatter(
                kv_weight_grad.astype(jnp.bfloat16), "dp", scatter_dimension=0, tiled=True
            ).astype(jnp.float32),
            lax.psum_scatter(
                value_bias_grad.astype(jnp.bfloat16), "dp", scatter_dimension=0, tiled=True
            ).astype(jnp.float32),
            lax.psum_scatter(
                out_weight_grad.astype(jnp.bfloat16), "dp", scatter_dimension=1, tiled=True
            ).astype(jnp.float32),
            lax.psum_scatter(
                out_bias_grad.astype(jnp.bfloat16), "dp", scatter_dimension=0, tiled=True
            ).astype(jnp.float32),
            lax.psum_scatter(
                mlp_gain_grad.astype(jnp.bfloat16), "dp", scatter_dimension=0, tiled=True
            ).astype(jnp.float32),
            lax.psum_scatter(
                mlp_shift_grad.astype(jnp.bfloat16), "dp", scatter_dimension=0, tiled=True
            ).astype(jnp.float32),
            lax.psum_scatter(
                up_weight_grad.astype(jnp.bfloat16), "dp", scatter_dimension=0, tiled=True
            ).astype(jnp.float32),
            lax.psum_scatter(
                up_bias_grad.astype(jnp.bfloat16), "dp", scatter_dimension=1, tiled=True
            ).astype(jnp.float32),
            lax.psum_scatter(
                down_weight_grad.astype(jnp.bfloat16), "dp", scatter_dimension=1, tiled=True
            ).astype(jnp.float32),
            lax.psum_scatter(
                down_bias_grad.astype(jnp.bfloat16), "dp", scatter_dimension=0, tiled=True
            ).astype(jnp.float32),
        )
    )
    return (output, input_grad) + summed


def solution(mesh):
    return jax.shard_map(
        body,
        mesh=mesh,
        in_specs=(
            P("dp", None),
            P("dp", None),
            P(),
            P("dp"),
            P("dp"),
            P("dp", "tensor"),
            P("tensor", "dp"),
            P("dp", None),
            P("dp"),
            P("tensor", "dp"),
            P("dp"),
            P("dp"),
            P("dp"),
            P("dp", "tensor"),
            P("tensor", "dp"),
            P("tensor", "dp"),
            P("dp"),
        ),
        out_specs=(
            P("dp", None),
            P("dp", None),
            P("dp"),
            P("dp"),
            P("dp", "tensor"),
            P("tensor", "dp"),
            P("dp", None),
            P("dp"),
            P("tensor", "dp"),
            P("dp"),
            P("dp"),
            P("dp"),
            P("dp", "tensor"),
            P("tensor", "dp"),
            P("tensor", "dp"),
            P("dp"),
        ),
        check_vma=False,
    )
```

profile of v0, /device:TPU:0, one launch (start us, length us, event | category | flops | bytes accessed | tf_op | source)
XLA Modules:
  0.0 1073.2 jit_solution(2823137192838508573)
XLA Ops:
  16.5 30.5 %all-reduce.2 = bf16[128]{0:T(256)(128)(2,1)S(1)} all-reduce(bf16[128]{0:T(256)(128)(2,1)S(1)} %dynamic-update-slice), channel_id=1, replica_groups=mesh['dp'=16,'tensor'=8] {'dp'}, use_global_device_ids=true, to_apply=%add.2 | all-reduce | flops 128 | bytes 512
  50.4 15.9 %all-gather.1 = bf16[16,1,128]{2,1,0:T(2,128)(2,1)S(1)} all-gather(bf16[1,1,128]{2,1,0:T(2,128)(2,1)S(1)} %convert_bitcast_fusion.5), channel_id=1, replica_groups=mesh['dp'=16,'tensor'=8] {'dp'}, dimensions={0}, use_global_device_ids=true | all-gather | bytes 4352 | tf_op jit(solution)/shard_map/all_gather | solution.py:95
  66.3 17.8 %all-gather = bf16[16,1,128]{2,1,0:T(2,128)(2,1)S(1)} all-gather(bf16[1,1,128]{2,1,0:T(2,128)(2,1)S(1)} %convert_bitcast_fusion.6), channel_id=1, replica_groups=mesh['dp'=16,'tensor'=8] {'dp'}, dimensions={0}, use_global_device_ids=true | all-gather | bytes 4352 | tf_op jit(solution)/shard_map/all_gather | solution.py:94
  99.5 23.1 %all-gather.2 = bf16[16,8,2]{1,2,0:T(2,128)(2,1)S(1)} all-gather(bf16[1,8,2]{1,2,0:T(2,128)(2,1)S(1)} %convert_bitcast_fusion.4), channel_id=1, replica_groups=mesh['dp'=16,'tensor'=8] {'dp'}, dimensions={0}, use_global_device_ids=true | all-gather | bytes 544 | tf_op jit(solution)/shard_map/all_gather | solution.py:97
  132.4 6.7 fusion.54
  139.1 7.0 exponential_reduce_fusion
  146.1 9.8 fusion.1
  173.6 16.2 %all-gather.5 = bf16[16,1,128]{2,1,0:T(2,128)(2,1)S(1)} all-gather(bf16[1,1,128]{2,1,0:T(2,128)(2,1)S(1)} %convert_bitcast_fusion.1), channel_id=1, replica_groups=mesh['dp'=16,'tensor'=8] {'dp'}, dimensions={0}, use_global_device_ids=true | all-gather | bytes 4352 | tf_op jit(solution)/shard_map/all_gather | solution.py:103
  191.1 17.5 %all-gather.4 = bf16[16,1,128]{2,1,0:T(2,128)(2,1)S(1)} all-gather(bf16[1,1,128]{2,1,0:T(2,128)(2,1)S(1)} %convert_bitcast_fusion.2), channel_id=1, replica_groups=mesh['dp'=16,'tensor'=8] {'dp'}, dimensions={0}, use_global_device_ids=true | all-gather | bytes 4352 | tf_op jit(solution)/shard_map/all_gather | solution.py:102
  209.8 16.2 %all-gather.3 = bf16[16,1,128]{2,1,0:T(2,128)(2,1)S(1)} all-gather(bf16[1,1,128]{2,1,0:T(2,128)(2,1)S(1)} %convert_bitcast_fusion.3), channel_id=1, replica_groups=mesh['dp'=16,'tensor'=8] {'dp'}, dimensions={0}, use_global_device_ids=true | all-gather | bytes 4352 | tf_op jit(solution)/shard_map/all_gather | solution.py:101
  226.6 19.9 %all_gather.53 = bf16[8,128]{0,1:T(8,128)(2,1)} all-gather(bf16[8,8]{0,1:T(8,128)(2,1)} %copy.55), channel_id=1, replica_groups=mesh['dp'=16,'tensor'=8] {'dp'}, dimensions={1}, use_global_device_ids=true | all-gather | bytes 2176 | tf_op jit(solution)/shard_map/all_gather | solution.py:105
  249.1 65.9 %all-reduce.18.cloned.1.call-done = f32[768,2048]{1,0:T(8,128)} async-done(((f32[768,2048]{1,0:T(8,128)}), f32[768,2048]{1,0:T(8,128)}) %all-reduce.18.cloned.1.call-update) | async-done | bytes 6291472 | tf_op jit(solution)/shard_map/psum | solution.py:150
  323.4 28.4 %all-gather.19.cloned.1.call-done = bf16[2048,1024]{1,0:T(8,128)(2,1)} async-done(((bf16[128,1024]{1,0:T(8,128)(2,1)}), bf16[2048,1024]{1,0:T(8,128)(2,1)}) %all-gather.19.cloned.1.call-update) | async-done | bytes 4194320 | tf_op jit(solution)/shard_map/all_gather | solution.py:104
  351.7 9.2 fusion.43
  360.9 37.9 %all-gather.21.cloned.1.call-done = bf16[1024,2048]{1,0:T(8,128)(2,1)} async-done(((bf16[1024,128]{1,0:T(8,128)(2,1)}), bf16[1024,2048]{1,0:T(8,128)(2,1)}) %all-gather.21.cloned.1.call-update) | async-done | bytes 4194320 | tf_op jit(solution)/shard_map/all_gather | solution.py:106
  398.8 10.6 fusion.45
  416.2 8.7 convolution_convert_fusion
  424.9 6.5 copy.65
  431.5 131.4 %all-reduce.20.cloned.1.call-done = f32[768,2048]{1,0:T(8,128)} async-done(((f32[768,2048]{1,0:T(8,128)}), f32[768,2048]{1,0:T(8,128)}) %all-reduce.20.cloned.1.call-update) | async-done | bytes 6291472 | tf_op jit(solution)/shard_map/psum | solution.py:166
  562.9 6.5 multiply_reduce_fusion.1
  582.5 9.2 convolution_convert_fusion.1
  597.3 13.0 %multiply_reduce_fusion = (f32[1536]{0:T(1024)S(1)}, f32[1536,2304]{1,0:T(8,128)}) fusion(f32[1536,2304]{1,0:T(8,128)} %get-tuple-element.49, f32[1536]{0:T(1024)S(1)} %log_add_fusion, bf16[1536,128]{1,0:T(8,128)(2,1)S(1)} %bitcast.99, bf16[2304,256]{1,0:T(8,128)(2,1)} %copy-done.10), kind=kOutput, calls=%fused_computation.3 | convolution fusion | flops 916584960 | bytes 29306880 | tf_op jit(solution)/shard_map/dot_general | solution.py:44
  611.6 7.3 multiply_convert_fusion
  643.5 7.5 convolution_convert_fusion.3
  653.8 6.0 collective-permute-done.3
  662.1 17.5 %all-gather.6 = bf16[16,1,128]{2,1,0:T(2,128)(2,1)S(1)} all-gather(bf16[1,1,128]{2,1,0:T(2,128)(2,1)S(1)} %convert_bitcast_fusion), channel_id=1, replica_groups=mesh['dp'=16,'tensor'=8] {'dp'}, dimensions={0}, use_global_device_ids=true | all-gather | bytes 4352 | tf_op jit(solution)/shard_map/all_gather | solution.py:107
  682.2 9.6 reduce-scatter.18.cloned.1.call-done
  693.4 66.8 %reduce-scatter.16.cloned.1.call-done = bf16[128,1024]{1,0:T(8,128)(2,1)} async-done(((bf16[2048,1024]{1,0:T(8,128)(2,1)}), bf16[128,1024]{1,0:T(8,128)(2,1)}) %reduce-scatter.16.cloned.1.call-update) | async-done | bytes 262160 | tf_op jit(solution)/shard_map/reduce_scatter | solution.py:236
  762.0 60.6 %reduce-scatter.12.cloned.1.call-done = bf16[128,256]{1,0:T(8,128)(2,1)} async-done(((bf16[2048,256]{1,0:T(8,128)(2,1)}), bf16[128,256]{1,0:T(8,128)(2,1)}) %reduce-scatter.12.cloned.1.call-update) | async-done | bytes 65552 | tf_op jit(solution)/shard_map/reduce_scatter | solution.py:212
  824.1 154.3 %all-reduce.22.cloned.1.call-done = (bf16[768,2048]{1,0:T(8,128)(2,1)}, bf16[768,2048]{1,0:T(8,128)(2,1)}, bf16[768,256]{0,1:T(8,128)(2,1)}) async-done(((bf16[768,2048]{1,0:T(8,128)(2,1)}, bf16[768,2048]{1,0:T(8,128)(2,1)}, bf16[768,256]{0,1:T(8,128)(2,1)}), (bf16[768,2048]{1,0:T(8,128)(2,1)}, bf16[768,2048]{1,0:T(8,128)(2,1)}, bf16[768,256]{0,1:T(8,128)(2,1)})) %all-reduce.22.cloned.1.call-update) | async-done | bytes 6684688 | tf_op jit(solution)/shard_map/psum | solution.py:157
  991.1 55.5 %all-reduce.12 = (bf16[2048]{0:T(1024)(128)(2,1)S(1)}, bf16[2048]{0:T(1024)(128)(2,1)S(1)}, bf16[2,128]{1,0:T(2,128)(2,1)S(1)}, bf16[128]{0:T(256)(128)(2,1)S(1)...) all-reduce(bf16[2048]{0:T(1024)(128)(2,1)S(1)} %get-tuple-element.1, ...), channel_id=2, replica_groups=mesh['dp'=16,'tensor'=8] {'dp'}, use_global_device_ids=true, to_apply=%region_17.18.clone | all-reduce | flops 13696 | bytes 54784
  1050.3 6.8 add_convert_fusion
  (232 shorter events, 156.5 us)
Async XLA Ops:
  7.2 42.2 %copy-start.1 = (bf16[768,2048]{1,0:T(8,128)(2,1)S(1)}, bf16[768,2048]{1,0:T(8,128)(2,1)}, u32[]{:S(2)}) copy-start(bf16[768,2048]{1,0:T(8,128)(2,1)} %param.17) | copy-start | bytes 9437188
  7.2 76.9 %copy-start.25 = (s32[12288]{0:T(1024)S(1)}, s32[12288]{0:T(1024)}, u32[]{:S(2)}) copy-start(s32[12288]{0:T(1024)} %param.19) | copy-start | bytes 147460
  7.2 83.4 %all-gather.15.cloned.1.call-start = ((), (), s32[]{:S(2)}) async-start(), calls=%async_computation.6 | async-start | bytes 1114112 | tf_op jit(solution)/shard_map/all_gather | solution.py:98
  9.0 114.0 %all-gather.13.cloned.1.call-start = ((), (), s32[]{:S(2)}) async-start(), calls=%async_computation.5 | async-start | bytes 1114112 | tf_op jit(solution)/shard_map/all_gather | solution.py:96
  10.6 152.3 %all-gather.17.cloned.1.call-start = ((), (), s32[]{:S(2)}) async-start(), calls=%async_computation.7 | async-start | bytes 1114112 | tf_op jit(solution)/shard_map/all_gather | solution.py:100
  12.2 302.8 %all-reduce.18.cloned.1.call-start = ((), (), s32[]{:S(2)}) async-start(), calls=%async_computation.8 | async-start | bytes 12582912 | tf_op jit(solution)/shard_map/psum | solution.py:150
  49.4 38.3 %copy-start.18 = (f32[768]{0:T(1024)}, f32[768]{0:T(1024)S(1)}, u32[]{:S(2)}) copy-start(f32[768]{0:T(1024)S(1)} %broadcast_multiply_fusion.1) | copy-start | bytes 9220
  50.4 37.3 %copy-start.27 = (f32[768]{0:T(1024)}, f32[768]{0:T(1024)S(1)}, u32[]{:S(2)}) copy-start(f32[768]{0:T(1024)S(1)} %fusion.12) | copy-start | bytes 9220
  50.4 37.3 %copy-start.23 = (f32[768]{0:T(1024)}, f32[768]{0:T(1024)S(1)}, u32[]{:S(2)}) copy-start(f32[768]{0:T(1024)S(1)} %fusion.37) | copy-start | bytes 9220
  94.5 33.6 %collective-permute-start.1 = (bf16[768,256]{1,0:T(8,128)(2,1)}, bf16[768,256]{1,0:T(8,128)(2,1)}, u32[]{:S(2)}, u32[]{:S(2)}) collective-permute-start(bf16[768,256]{1,0:T(8,128)(2,1)} %fusion.27), channel_id=1, source_target_pairs={{0,8},{8,16},{16,24},{24,32},{32,40},{40,48},{48,56},{56,64},{64,7... | collective-permute-start | bytes 1179656 | tf_op jit(solution)/shard_map/ppermute | solution.py:19
  97.5 30.6 %collective-permute-start = (bf16[768,256]{1,0:T(8,128)(2,1)}, bf16[768,256]{1,0:T(8,128)(2,1)}, u32[]{:S(2)}, u32[]{:S(2)}) collective-permute-start(bf16[768,256]{1,0:T(8,128)(2,1)} %fusion.27), channel_id=1, source_target_pairs={{0,16},{8,24},{16,32},{24,40},{32,48},{40,56},{48,64},{56,72},{64,... | collective-permute-start | bytes 1179656 | tf_op jit(solution)/shard_map/ppermute | solution.py:19
  128.1 11.0 %copy-start.13 = (bf16[768,2,128]{2,0,1:T(8,128)(2,1)}, bf16[768,2,128]{2,0,1:T(8,128)(2,1)S(1)}, u32[]{:S(2)}) copy-start(bf16[768,2,128]{2,0,1:T(8,128)(2,1)S(1)} %copy.53) | copy-start | bytes 1179652
  129.6 9.5 copy-start.10
  167.9 183.9 %all-gather.19.cloned.1.call-start = ((), (), s32[]{:S(2)}) async-start(), calls=%async_computation.9 | async-start | bytes 4456448 | tf_op jit(solution)/shard_map/all_gather | solution.py:104
  169.7 229.1 %all-gather.21.cloned.1.call-start = ((), (), s32[]{:S(2)}) async-start(), calls=%async_computation.10 | async-start | bytes 4456448 | tf_op jit(solution)/shard_map/all_gather | solution.py:106
  171.6 391.3 %all-reduce.20.cloned.1.call-start = ((), (), s32[]{:S(2)}) async-start(), calls=%async_computation.11 | async-start | bytes 12582912 | tf_op jit(solution)/shard_map/psum | solution.py:166
  398.8 11.7 %copy-start.41 = (bf16[2048,1024]{1,0:T(8,128)(2,1)S(1)}, bf16[2048,1024]{1,0:T(8,128)(2,1)}, u32[]{:S(2)}) copy-start(bf16[2048,1024]{1,0:T(8,128)(2,1)} %all-gather.19.cloned.1.call-done) | copy-start | bytes 12582916
  415.9 264.3 %reduce-scatter.20.cloned.1.call-start = ((), (), s32[]{:S(2)}) async-start(), calls=%async_computation.16 | async-start | bytes 4456448
  431.4 260.3 %reduce-scatter.18.cloned.1.call-start = ((), (), s32[]{:S(2)}) async-start(), calls=%async_computation.15 | async-start | bytes 1114112
  582.5 177.7 %reduce-scatter.16.cloned.1.call-start = ((), (), s32[]{:S(2)}) async-start(), calls=%async_computation.14 | async-start | bytes 4456448 | tf_op jit(solution)/shard_map/reduce_scatter | solution.py:236
  591.7 230.8 %reduce-scatter.12.cloned.1.call-start = ((), (), s32[]{:S(2)}) async-start(), calls=%async_computation.12 | async-start | bytes 1114112 | tf_op jit(solution)/shard_map/reduce_scatter | solution.py:212
  597.2 13.1 %slice-start = ((s8[14155776]{0:T(1024)(128)(4,1)}), s8[4194304]{0:T(1024)(128)(4,1)S(1)}, s32[]{:S(2)}) async-start(s8[14155776]{0:T(1024)(128)(4,1)} %bitcast.92), calls=%async_computation.18 | async-start | bytes 8388608
  597.2 13.1 %slice-start.1 = ((s8[14155776]{0:T(1024)(128)(4,1)}), s8[4194304]{0:T(1024)(128)(4,1)S(1)}, s32[]{:S(2)}) async-start(s8[14155776]{0:T(1024)(128)(4,1)} %bitcast.92), calls=%async_computation.19 | async-start | bytes 8388608
  597.2 13.8 %slice-start.2 = ((s8[14155776]{0:T(1024)(128)(4,1)}), s8[4194304]{0:T(1024)(128)(4,1)S(1)}, s32[]{:S(2)}) async-start(s8[14155776]{0:T(1024)(128)(4,1)} %bitcast.92), calls=%async_computation.20 | async-start | bytes 8388608
  597.3 14.4 %slice-start.3 = ((s8[14155776]{0:T(1024)(128)(4,1)}), s8[1572864]{0:T(1024)(128)(4,1)S(1)}, s32[]{:S(2)}) async-start(s8[14155776]{0:T(1024)(128)(4,1)} %bitcast.92), calls=%async_computation.21 | async-start | bytes 3145728
  638.5 339.9 %all-reduce.22.cloned.1.call-start = ((), (), s32[]{:S(2)}) async-start(), calls=%async_computation.17 | async-start | bytes 13369344 | tf_op jit(solution)/shard_map/psum | solution.py:157
  640.5 13.3 %collective-permute-start.2 = (bf16[768,256]{0,1:T(8,128)(2,1)S(1)}, bf16[768,256]{0,1:T(8,128)(2,1)S(1)}, u32[]{:S(2)}, u32[]{:S(2)}) collective-permute-start(bf16[768,256]{0,1:T(8,128)(2,1)S(1)} %get-tuple-element.44), channel_id=1, source_target_pairs={{8,0},{16,8},{24,16},{32,24},{40,32},{48,40},{56,48},{64,56},{72,6... | collective-permute-start | bytes 1179656 | tf_op jit(solution)/shard_map/ppermute | solution.py:19
  641.8 9.2 copy-start.16
  641.8 17.9 %collective-permute-start.3 = (bf16[768,256]{0,1:T(8,128)(2,1)S(1)}, bf16[768,256]{0,1:T(8,128)(2,1)S(1)}, u32[]{:S(2)}, u32[]{:S(2)}) collective-permute-start(bf16[768,256]{0,1:T(8,128)(2,1)S(1)} %get-tuple-element.45), channel_id=1, source_target_pairs={{16,0},{24,8},{32,16},{40,24},{48,32},{56,40},{64,48},{72,56},{80,... | collective-permute-start | bytes 1179656 | tf_op jit(solution)/shard_map/ppermute | solution.py:19
  660.6 18.9 %copy-start.15 = (bf16[1536,128]{1,0:T(8,128)(2,1)S(1)}, bf16[1536,128]{1,0:T(8,128)(2,1)}, u32[]{:S(2)}) copy-start(bf16[1536,128]{1,0:T(8,128)(2,1)} %fusion.24) | copy-start | bytes 1179652
  660.7 404.0 %reduce-scatter.14.cloned.1.call-start = ((), (), s32[]{:S(2)}) async-start(), calls=%async_computation.13 | async-start | bytes 1114112 | tf_op jit(solution)/shard_map/reduce_scatter | solution.py:218
  762.0 221.4 %copy-start.19 = (f32[768]{0:T(1024)S(1)}, f32[768]{0:T(1024)}, u32[]{:S(2)}) copy-start(f32[768]{0:T(1024)} %copy-done.18) | copy-start | bytes 9220
  (36 other events, 175.7 us)
Sparse Core Ops, SparseCore 0:
  10.3 34.8 all-gather.14
  47.5 32.4 all-gather.12
  82.2 38.0 all-gather.16
  168.0 146.9 all-reduce.17
  317.2 34.5 all-gather.18
  353.8 44.9 all-gather.20
  416.1 146.8 all-reduce.19
  565.3 64.0 reduce-scatter.19
  631.8 59.9 reduce-scatter.17
  694.1 66.0 reduce-scatter.15
  762.7 59.8 reduce-scatter.11
  825.2 153.0 all-reduce.21
  983.5 58.6 reduce-scatter.13
where the time goes:
time: 1080 us; the launch traced here: 1070 us
  waiting for transfers between devices  561 us (52%)
  blocking collectives  230 us (21%)
  matrix products  124 us (11%)
  other arithmetic  99.1 us (9%)
  local copies, waits for them, and re-layouts  33.2 us (3%)
  between operations  17.2 us (2%)
    psum x1, waiting for transfers between devices, body(): lax.psum(matmul(hidden, down_w).astype(jnp.bfloat16), 'tensor')  154 us
    psum x1, waiting for transfers between devices, body(): grad_norm_two = lax.psum(contract_cols(grad_up, up_w), 'tensor')  131 us
    unnamed x2, blocking collectives  86 us
    reduce_scatter x1, waiting for transfers between devices, body(): lax.psum_scatter(up_weight_grad.astype(jnp.bfloat16), 'dp', scatter_dimen...  66.8 us
    psum x1, waiting for transfers between devices, body(): middle = inputs + lax.psum(matmul(attended, out_w), 'tensor') + out_b  65.9 us
    reduce_scatter x1, waiting for transfers between devices, body(): lax.psum_scatter(query_weight_grad.astype(jnp.bfloat16), 'dp', scatter_di...  60.6 us
    dot_general x7, matrix products, contract_cols(): lax.dot_general(left, right, (((1,), (1,)), ((), ())), preferred_element_...  47.1 us
    dot_general x7, matrix products, matmul(): return jnp.dot(left, right, preferred_element_type=jnp.float32)  38.4 us
  transfers between devices with their start and end apart: 17, of which 9 were waited for; matrix products, arithmetic and copies ran while one was open for 20% of the time, Pallas kernels for 0%

commit v1 on v0

v1 whole, which is shorter than its diff:
```python
import functools
import math

import jax
import jax.numpy as jnp
from jax import lax
from jax.experimental import pallas as pl
from jax.experimental.pallas import tpu as pltpu
from jax.sharding import PartitionSpec as P

HD = 128
EPS = 1e-05
NEG = -1e30
MESH = pl.DeviceIdType.MESH
bf16 = jnp.bfloat16
f32 = jnp.float32


class Place:
    def __init__(self):
        dp = lax.axis_index("dp")
        tensor = lax.axis_index("tensor")
        self.core = dp % 2
        self.x = (dp // 2) % 4
        self.y = (tensor // 4) * 2 + dp // 8
        self.z = tensor % 4

    def dev(self, x=None, y=None, z=None, core=None):
        x = self.x if x is None else x
        y = self.y if y is None else y
        z = self.z if z is None else z
        core = self.core if core is None else core
        return ((y % 2) * 8 + x * 2 + core, (y // 2) * 4 + z)

    def sibling(self):
        return self.dev(core=1 - self.core)

    def ring(self, axis):
        return Ring(self, axis)


class Ring:
    def __init__(self, place, axis):
        self.p = getattr(place, axis)
        self.plus = place.dev(**{axis: (self.p + 1) % 4})
        self.minus = place.dev(**{axis: (self.p + 3) % 4})
        self.after = (self.p + 1) % 4
        self.before = (self.p + 3) % 4
        self.across = (self.p + 2) % 4


class Net:
    def __init__(self, ssem, rsem, lsem):
        self.ssem, self.rsem, self.lsem = ssem, rsem, lsem
        self.n = 0
        self.m = 0
        self.sent = []
        self.todo = []

    def send(self, src, dst, dev):
        i = self.n
        self.n += 1
        copy = pltpu.make_async_remote_copy(
            src_ref=src,
            dst_ref=dst,
            send_sem=self.ssem.at[i],
            recv_sem=self.rsem.at[i],
            device_id=dev,
            device_id_type=MESH,
        )
        copy.start()
        self.sent.append(copy)
        return copy

    def local(self, src, dst):
        i = self.m
        self.m += 1
        copy = pltpu.make_async_copy(src, dst, self.lsem.at[i])
        copy.start()
        return copy

    def run(self, *gens):
        self.todo.extend(gens)
        while self.todo:
            for gen in list(self.todo):
                try:
                    next(gen)
                except StopIteration:
                    self.todo.remove(gen)
        for copy in self.sent:
            copy.wait_send()


def greet(devices):
    barrier = pltpu.get_barrier_semaphore()
    for device in devices:
        pl.semaphore_signal(barrier, inc=1, device_id=device, device_id_type=MESH)
    pl.semaphore_wait(barrier, len(devices))


def rows_half(ref, which):
    n = ref.shape[-2] // 2
    if len(ref.shape) == 2:
        return ref.at[pl.ds(which * n, n), :]
    return ref.at[:, pl.ds(which * n, n), :]


def lane_step(shape):
    return max(16, min(shape[0], 32768 // shape[1]))


def over_rows(rows, step, fn):
    def one(i, carry):
        fn(pl.ds(pl.multiple_of(i * step, step), step))
        return carry

    lax.fori_loop(0, rows // step, one, 0)


def add_into(dst, *srcs, out=None):
    out = dst if out is None else out
    rows, step = dst.shape[0], lane_step(dst.shape)
    if rows % step:
        step = 16 if rows % 16 == 0 else rows

    def one(at):
        total = dst[at, :].astype(f32)
        for src in srcs:
            total = total + src[at, :].astype(f32)
        out[at, :] = total.astype(out.dtype)

    over_rows(rows, step, one)


def ag_ring(net, ring, slot, own, have=None):
    have = have or (lambda pos: None)
    c0 = net.send(own, slot(ring.p), ring.plus)
    c1 = net.send(own, slot(ring.p), ring.minus)
    yield
    c0.wait_recv()
    one = rows_half(slot(ring.before), 0)
    c2 = net.send(one, one, ring.plus)
    have(ring.before)
    c1.wait_recv()
    two = rows_half(slot(ring.after), 1)
    c3 = net.send(two, two, ring.minus)
    have(ring.after)
    yield
    c2.wait_recv()
    c3.wait_recv()
    have(ring.across)


def ag2d(net, place, own, slot, first, second):
    sib = place.sibling()
    pairs = []

    def give(a, b, src=None):
        ref = slot(a, b)
        pairs.append(net.send(ref if src is None else src, ref, sib))

    def column(a, src):
        return ag_ring(net, second, lambda b: slot(a, b), src, lambda b: give(a, b))

    def main():
        keep = net.local(own, slot(first.p, second.p))
        c0 = net.send(own, slot(first.p, second.p), first.plus)
        c1 = net.send(own, slot(first.p, second.p), first.minus)
        net.todo.append(column(first.p, own))
        give(first.p, second.p, own)
        yield
        c0.wait_recv()
        one = rows_half(slot(first.before, second.p), 0)
        c2 = net.send(one, one, first.plus)
        net.todo.append(column(first.before, slot(first.before, second.p)))
        c1.wait_recv()
        two = rows_half(slot(first.after, second.p), 1)
        c3 = net.send(two, two, first.minus)
        net.todo.append(column(first.after, slot(first.after, second.p)))
        give(first.before, second.p)
        give(first.after, second.p)
        yield
        c2.wait_recv()
        c3.wait_recv()
        net.todo.append(column(first.across, slot(first.across, second.p)))
        give(first.across, second.p)
        keep.wait()
        while len(pairs) < 16:
            yield
        for pair in pairs:
            pair.wait_recv()

    return main()


def rs_ring(net, ring, src, ra, rb, done):
    across, after, before = src(ring.across), src(ring.after), src(ring.before)
    a0 = net.send(rows_half(across, 0), ra(0), ring.plus)
    a1 = net.send(rows_half(across, 1), ra(1), ring.minus)
    b0 = net.send(rows_half(after, 1), rows_half(rb(0), 1), ring.plus)
    b1 = net.send(rows_half(before, 0), rows_half(rb(1), 0), ring.minus)
    yield
    a0.wait_recv()
    add_into(ra(0), rows_half(after, 0))
    b2 = net.send(ra(0), rows_half(rb(0), 0), ring.plus)
    a1.wait_recv()
    add_into(ra(1), rows_half(before, 1))
    b3 = net.send(ra(1), rows_half(rb(1), 1), ring.minus)
    yield
    for copy in (b0, b1, b2, b3):
        copy.wait_recv()
    done(src(ring.p), rb(0), rb(1))


def rs2d(net, place, part, first, second, bufs, out):
    r0, rv, ra, rb, r1, sa, sb = bufs
    sib = place.sibling()
    firsts = (first.across, first.after, first.before, first.p)
    seconds = (second.across, second.after, second.before, second.p)
    come, keep = {}, {}
    for i, a in enumerate(firsts):
        for j, b in enumerate(seconds):
            come[i, j] = net.send(part(a, b, 1 - place.core), rv.at[i, j], sib)
            keep[i, j] = net.local(part(a, b, place.core), r0.at[i, j])

    def pair(i, j):
        come[i, j].wait_recv()
        keep[i, j].wait()
        add_into(r0.at[i, j], rv.at[i, j])

    yield
    halves, wholes = {}, {}
    for j in range(4):
        pair(0, j)
        halves[0, j] = net.send(rows_half(r0.at[0, j], 0), ra.at[0, j], first.plus)
        halves[1, j] = net.send(rows_half(r0.at[0, j], 1), ra.at[1, j], first.minus)
    yield
    for j in range(4):
        pair(1, j)
        wholes[0, j] = net.send(rows_half(r0.at[1, j], 1), rows_half(rb.at[0, j], 1), first.plus)
        pair(2, j)
        wholes[1, j] = net.send(rows_half(r0.at[2, j], 0), rows_half(rb.at[1, j], 0), first.minus)
    yield
    for j in range(4):
        halves[0, j].wait_recv()
        add_into(ra.at[0, j], rows_half(r0.at[1, j], 0))
        wholes[2, j] = net.send(ra.at[0, j], rows_half(rb.at[0, j], 0), first.plus)
        halves[1, j].wait_recv()
        add_into(ra.at[1, j], rows_half(r0.at[2, j], 1))
        wholes[3, j] = net.send(ra.at[1, j], rows_half(rb.at[1, j], 1), first.minus)
        pair(3, j)
    yield

    def settle(j):
        for k in range(4):
            wholes[k, j].wait_recv()
        add_into(r0.at[3, j], rb.at[0, j], rb.at[1, j], out=r1.at[j])

    settle(0)
    a0 = net.send(rows_half(r1.at[0], 0), sa.at[0], second.plus)
    a1 = net.send(rows_half(r1.at[0], 1), sa.at[1], second.minus)
    settle(1)
    b0 = net.send(rows_half(r1.at[1], 1), rows_half(sb.at[0], 1), second.plus)
    settle(2)
    b1 = net.send(rows_half(r1.at[2], 0), rows_half(sb.at[1], 0), second.minus)
    settle(3)
    yield
    a0.wait_recv()
    add_into(sa.at[0], rows_half(r1.at[1], 0))
    b2 = net.send(sa.at[0], rows_half(sb.at[0], 0), second.plus)
    a1.wait_recv()
    add_into(sa.at[1], rows_half(r1.at[2], 1))
    b3 = net.send(sa.at[1], rows_half(sb.at[1], 1), second.minus)
    yield
    for copy in (b0, b1, b2, b3):
        copy.wait_recv()
    add_into(r1.at[3], sb.at[0], sb.at[1], out=out)


def rs2d_bufs(shape, dtype=bf16):
    rows, cols = shape
    half = (rows // 2, cols)
    return [
        pltpu.VMEM((4, 4) + shape, dtype),
        pltpu.VMEM((4, 4) + shape, dtype),
        pltpu.VMEM((2, 4) + half, dtype),
        pltpu.VMEM((2, 4) + shape, dtype),
        pltpu.VMEM((4,) + shape, dtype),
        pltpu.VMEM((2,) + half, dtype),
        pltpu.VMEM((2,) + shape, dtype),
    ]


def sems(count, local):
    return [
        pltpu.SemaphoreType.DMA((count,)),
        pltpu.SemaphoreType.DMA((count,)),
        pltpu.SemaphoreType.DMA((local,)),
    ]


ANY = pl.BlockSpec(memory_space=pl.ANY)
VM = pl.BlockSpec(memory_space=pltpu.VMEM)


def kernel_call(body, name, cid, ins, in_specs, outs, out_specs, scratch, nbytes=1 << 20):
    return pl.pallas_call(
        body,
        out_shape=[jax.ShapeDtypeStruct(s, d) for s, d in outs],
        in_specs=in_specs,
        out_specs=out_specs,
        scratch_shapes=scratch,
        compiler_params=pltpu.CompilerParams(
            collective_id=cid, has_side_effects=True, vmem_limit_bytes=56 << 20
        ),
        cost_estimate=pl.CostEstimate(flops=0, bytes_accessed=nbytes, transcendentals=0),
        name=name,
    )(*ins)


def block_of(x, y, core):
    return (y % 2) * 8 + x * 2 + core


def col_at(d):
    return pl.ds(pl.multiple_of(d * 128, 128), 128)


def row_at(start, size):
    return pl.ds(pl.multiple_of(start, size), size)


def at_query(ref, x, y, core):
    return ref.at[row_at(block_of(x, y, core) * 128, 128), row_at((y // 2) * 256, 256)]


def at_keyval(ref, x, y, core):
    return ref.at[row_at(block_of(x, y, core) * 128 + (y // 2) * 64, 64), :]


def at_out(ref, x, y, core):
    return ref.at[row_at((y // 2) * 256, 256), col_at(block_of(x, y, core))]


def at_up(ref, x, y, core):
    return ref.at[row_at(block_of(x, y, core) * 128, 128), row_at((y // 2) * 1024, 1024)]


def at_down(ref, x, y, core):
    return ref.at[row_at((y // 2) * 1024, 1024), col_at(block_of(x, y, core))]


def at_small(ref, x, y, core):
    return ref.at[y // 2, block_of(x, y, core)]


def gather(net, place, at, own, whole, order):
    x, y = place.ring("x"), place.ring("y")
    if order == "xy":
        return ag2d(net, place, own, lambda a, b: at(whole, a, b, place.core), x, y)
    return ag2d(net, place, own, lambda a, b: at(whole, b, a, place.core), y, x)


def scatter(net, place, at, part, order, bufs, out):
    x, y = place.ring("x"), place.ring("y")
    if order == "xy":
        return rs2d(net, place, lambda a, b, c: at(part, a, b, c), x, y, bufs, out)
    return rs2d(net, place, lambda a, b, c: at(part, b, a, c), y, x, bufs, out)


def plane_peers(place):
    x, y = place.ring("x"), place.ring("y")
    return [place.sibling(), x.plus, x.minus, y.plus, y.minus]


def gather_first(query_w, keyval_w, out_w, small, g_query, g_keyval, g_out, g_small, *sem):
    place = Place()
    greet(plane_peers(place))
    net = Net(*sem)
    net.run(
        gather(net, place, at_query, query_w, g_query, "xy"),
        gather(net, place, at_out, out_w, g_out, "yx"),
        gather(net, place, at_keyval, keyval_w, g_keyval, "xy"),
        gather(net, place, at_small, small, g_small, "yx"),
    )


def spread(values):
    center = values - jnp.mean(values, axis=-1, keepdims=True)
    return center, lax.rsqrt(jnp.mean(center * center, axis=-1, keepdims=True) + EPS)


def attn_out(part, tok, vecs, up_w, down_w, g_up, g_down, normed, middle, ra, rb, mine, *sem):
    place = Place()
    z = place.ring("z")
    greet(plane_peers(place) + [z.plus, z.minus])
    net = Net(*sem)

    def rows():
        def done(own, one, two):
            def some(at):
                mid = (
                    tok[at, :].astype(f32)
                    + own[at, :].astype(f32)
                    + one[at, :].astype(f32)
                    + two[at, :].astype(f32)
                    + vecs[0:1, :]
                )
                middle[at, :] = mid
                center, inv = spread(mid)
                mine[at, :] = (center * inv * vecs[1:2, :] + vecs[2:3, :]).astype(bf16)

            over_rows(96, 16, some)

        yield from rs_ring(net, z, lambda i: part.at[i], lambda i: ra.at[i], lambda i: rb.at[i], done)
        keep = net.local(mine, normed.at[z.p])
        yield from ag_ring(net, z, lambda i: normed.at[i], mine)
        keep.wait()

    net.run(
        rows(),
        gather(net, place, at_up, up_w, g_up, "xy"),
        gather(net, place, at_down, down_w, g_down, "yx"),
    )


def mlp_back(
    part_out, part_norm, middle, cot, vecs, part_up, part_down,
    out_rows, grad_mid, grad_all, sums, up_grad, down_grad,
    ra, rb, rc, rd, mine, *rest,
):
    place = Place()
    z = place.ring("z")
    greet(plane_peers(place) + [z.plus, z.minus])
    ups, downs, sem = rest[:7], rest[7:14], rest[14:]
    net = Net(*sem)

    def back():
        def done(own, one, two):
            sums[...] = jnp.zeros_like(sums)

            def some(at):
                grad = own[at, :].astype(f32) + one[at, :].astype(f32) + two[at, :].astype(f32)
                center, inv = spread(middle[at, :])
                norm = center * inv
                flow = grad * vecs[1:2, :]
                top = cot[at, :].astype(f32)
                mid = top + inv * (
                    flow
                    - jnp.mean(flow, axis=-1, keepdims=True)
                    - norm * jnp.mean(flow * norm, axis=-1, keepdims=True)
                )
                grad_mid[at, :] = mid
                low = mid.astype(bf16)
                mine[at, :] = low
                sums[0:1, :] += jnp.sum(grad * norm, axis=0, keepdims=True)
                sums[1:2, :] += jnp.sum(grad, axis=0, keepdims=True)
                sums[2:3, :] += jnp.sum(low.astype(f32), axis=0, keepdims=True)
                sums[3:4, :] += jnp.sum(top, axis=0, keepdims=True)

            over_rows(96, 16, some)

        yield from rs_ring(
            net, z, lambda i: part_norm.at[i], lambda i: ra.at[i], lambda i: rb.at[i], done
        )
        keep = net.local(mine, grad_all.at[z.p])
        yield from ag_ring(net, z, lambda i: grad_all.at[i], mine)
        keep.wait()

    def fore():
        def done(own, one, two):
            def some(at):
                out_rows[at, :] = (
                    middle[at, :]
                    + own[at, :].astype(f32)
                    + one[at, :].astype(f32)
                    + two[at, :].astype(f32)
                    + vecs[0:1, :]
                ).astype(bf16)

            over_rows(96, 16, some)

        yield
        yield from rs_ring(
            net, z, lambda i: part_out.at[i], lambda i: rc.at[i], lambda i: rd.at[i], done
        )

    net.run(
        back(),
        scatter(net, place, at_up, part_up, "yx", ups, up_grad),
        scatter(net, place, at_down, part_down, "xy", downs, down_grad),
        fore(),
    )


def device_of_block(place, block):
    d = block // 2
    return ((d // 8) * 8 + ((d // 2) % 4) * 2 + d % 2, (block % 2) * 4 + place.z)


def attn_back(pieces, part, kv_grad, total, ra, rb, rk, stage, rz, *sem):
    place = Place()
    z = place.ring("z")
    peers = [place.dev(z=(place.z + k) % 4) for k in (1, 2, 3)]
    block = ((place.y % 2) * 8 + place.x * 2 + place.core) * 2 + place.y // 2
    earlier = [device_of_block(place, (block + 32 - k) % 32) for k in (1, 2, 3, 4)]
    later = [device_of_block(place, (block + k) % 32) for k in (1, 2, 3, 4)]
    greet(peers + earlier + later)
    net = Net(*sem)

    def kv():
        sent = [net.send(pieces.at[4 - k], rk.at[k - 1], earlier[k - 1]) for k in (1, 2, 3, 4)]
        yield
        for copy in sent:
            copy.wait_recv()
        for i in range(4):
            at = pl.ds(i * 96, 96)
            add_into(
                pieces.at[4, at], *[rk.at[k, at] for k in range(4)], out=stage.at[i]
            )
        out = [net.send(stage.at[(place.z + k) % 4], rz.at[k - 1], peers[k - 1]) for k in (1, 2, 3)]
        yield
        for copy in out:
            copy.wait_recv()
        add_into(stage.at[place.z], *[rz.at[k] for k in range(3)], out=kv_grad.at[place.z])
        home = kv_grad.at[place.z]
        out = [net.send(home, home, peer) for peer in peers]
        yield
        for copy in out:
            copy.wait_recv()

    def done(own, one, two):
        add_into(own, one, two, out=total)

    net.run(
        kv(),
        rs_ring(net, z, lambda i: part.at[i], lambda i: ra.at[i], lambda i: rb.at[i], done),
    )


def finish(
    out_rows, in_rows, part_query, part_keyval, part_out, part_small,
    output, input_grad, query_grad, keyval_grad, out_grad, small_grad,
    small_own, small_in, kv_own, *rest,
):
    place = Place()
    x, y, z = place.ring("x"), place.ring("y"), place.ring("z")
    partner = place.dev(y=y.across)
    across = place.dev(z=z.across)
    greet(plane_peers(place) + [z.plus, z.minus, partner, across])
    hi = place.y // 2
    queries, keyvals, outs, smalls, sem = (
        rest[:7], rest[7:14], rest[14:21], rest[21:28], rest[28:],
    )
    net = Net(*sem)

    def y_first(own, whole):
        keep = net.local(own, whole.at[hi, z.p])
        swap = net.send(own, whole.at[hi, z.p], partner)
        net.todo.append(ag_ring(net, z, lambda i: whole.at[hi, i], own))
        yield
        swap.wait_recv()
        net.todo.append(ag_ring(net, z, lambda i: whole.at[1 - hi, i], whole.at[1 - hi, z.p]))
        yield
        keep.wait()

    def z_first(own, whole):
        keep = net.local(own, whole.at[hi, z.p])
        swaps = [net.send(own, whole.at[hi, z.p], partner)]

        def have(i):
            ref = whole.at[hi, i]
            swaps.append(net.send(ref, ref, partner))

        yield from ag_ring(net, z, lambda i: whole.at[hi, i], own, have)
        yield
        keep.wait()
        for swap in swaps:
            swap.wait_recv()

    def keyval():
        yield from scatter(net, place, at_keyval, part_keyval, "yx", keyvals, kv_own)
        home = keyval_grad.at[pl.ds(pl.multiple_of(hi * 64, 64), 64), :]
        keep = net.local(kv_own, home)
        swap = net.send(kv_own, home, partner)
        yield
        keep.wait()
        swap.wait_recv()

    def small():
        yield from scatter(net, place, at_small, part_small, "xy", smalls, small_own)
        sent = [
            net.send(small_own, small_in.at[0], z.plus),
            net.send(small_own, small_in.at[1], z.minus),
            net.send(small_own, small_in.at[2], across),
        ]
        yield
        for copy in sent:
            copy.wait_recv()
        total = small_own[...]
        whole = total + small_in[0] + small_in[1] + small_in[2]
        row = lax.broadcasted_iota(jnp.int32, (16, 128), 0)
        small_grad[...] = jnp.where(row < 6, whole, total)

    net.run(
        z_first(in_rows, input_grad),
        small(),
        keyval(),
        y_first(out_rows, output),
        scatter(net, place, at_query, part_query, "xy", queries, query_grad),
        scatter(net, place, at_out, part_out, "yx", outs, out_grad),
    )


def matmul(left, right):
    return jnp.dot(left, right, preferred_element_type=f32)


def contract_rows(left, right):
    return lax.dot_general(left, right, (((0,), (0,)), ((), ())), preferred_element_type=f32)


def contract_cols(left, right):
    return lax.dot_general(left, right, (((1,), (1,)), ((), ())), preferred_element_type=f32)


def gelu_tanh(upward):
    inner = 0.7978845608028654 * (upward + 0.044715 * upward * upward * upward)
    return 0.5 * upward * (1.0 + jnp.tanh(inner))


def from_behind(value, axis, steps):
    count = lax.axis_size(axis)
    return lax.ppermute(value, axis, [(source, source + steps) for source in range(count - steps)])


def heads_to_rows(matrix, heads, rows):
    return matrix.reshape(rows, heads, HD).transpose(1, 0, 2).reshape(heads * rows, HD)


def rows_to_heads(matrix, heads, rows):
    return matrix.reshape(heads, rows, HD).transpose(1, 0, 2).reshape(rows, heads * HD)


def body(
    tokens, cotangent, segments, attn_norm_gain, attn_norm_bias, query_weight, query_bias,
    kv_weight, value_bias, out_weight, out_bias, mlp_norm_gain, mlp_norm_bias, up_weight,
    up_bias, down_weight, down_bias,
):
    dp = lax.axis_index("dp")
    tensor = lax.axis_index("tensor")
    hi, z = tensor // 4, tensor % 4
    scale = 1.0 / math.sqrt(HD)
    half, heads = 384, 4

    rest = jnp.concatenate([query_bias.reshape(-1), up_bias.reshape(-1), value_bias.reshape(-1)])
    small = jnp.stack(
        [attn_norm_gain, attn_norm_bias, out_bias, mlp_norm_gain, mlp_norm_bias, down_bias,
         jnp.pad(rest, (0, 40))]
    )
    small = jnp.pad(small, ((0, 9), (0, 0))).astype(bf16).astype(f32)
    keyval_own = lax.dynamic_slice_in_dim(kv_weight, hi * 64, 64).astype(bf16)
    query_w, keyval_w, out_w, small_all = kernel_call(
        gather_first, "gather_first", 0,
        [query_weight.astype(bf16), keyval_own, out_weight.astype(bf16), small],
        [ANY] * 4,
        [((2048, 512), bf16), ((2048, 256), bf16), ((512, 2048), bf16), ((2, 16, 16, 128), f32)],
        [ANY] * 4,
        sems(160, 8),
    )
    vectors = small_all[0, :, :6].transpose(1, 0, 2).reshape(6, 2048)
    gain_one, shift_one, out_b, gain_two, shift_two, down_b = (vectors[i] for i in range(6))
    others = small_all[:, :, 6]
    query_b = others[:, :, :16].reshape(2, 16, 2, 8).transpose(0, 2, 1, 3).reshape(512)
    up_b = others[:, :, 16:80].reshape(2, 16, 8, 8).transpose(0, 2, 1, 3).reshape(2048)
    value_b = others[0, :, 80:88].reshape(128)

    center, inv = spread(tokens.astype(f32))
    normed_all = (center * inv * gain_one + shift_one).astype(bf16)
    normed_one = lax.dynamic_slice_in_dim(normed_all, hi * half, half)
    keyval = (
        matmul(normed_all, keyval_w) + jnp.concatenate([jnp.zeros((HD,), f32), value_b])
    ).astype(bf16)
    query = (matmul(normed_one, query_w) + query_b).astype(bf16)
    window = jnp.concatenate([from_behind(keyval, "dp", 2), from_behind(keyval, "dp", 1), keyval])
    window = lax.dynamic_slice_in_dim(window, hi * half, 5 * half)
    keys, values = window[:, :HD], window[:, HD:]
    start = dp * 768 + hi * half
    key_seg = lax.dynamic_slice_in_dim(
        jnp.concatenate([jnp.full((4 * half,), -1, jnp.int32), segments]), start, 5 * half
    )
    query_seg = lax.dynamic_slice_in_dim(segments, start, half)
    allowed = (query_seg[:, None] == key_seg[None, :]) & (
        jnp.arange(5 * half)[None, :] <= 4 * half + jnp.arange(half)[:, None]
    )
    allowed = jnp.tile(allowed, (heads, 1))
    query_rows = heads_to_rows(query, heads, half)
    scores = jnp.where(allowed, contract_cols(query_rows, keys) * scale, NEG)
    top = jnp.max(scores, axis=-1, keepdims=True)
    log_total = top + jnp.log(jnp.sum(jnp.exp(scores - top), axis=-1, keepdims=True))
    probs = jnp.exp(scores - log_total).astype(bf16)
    attended = rows_to_heads(matmul(probs, values).astype(bf16), heads, half)
    attn_part = matmul(attended, out_w).astype(bf16).reshape(4, 96, 2048)

    mine = hi * half + z * 96
    tok_rows = lax.dynamic_slice_in_dim(tokens, mine, 96)
    cot_rows = lax.dynamic_slice_in_dim(cotangent, mine, 96)
    up_w, down_w, normed_two, middle = kernel_call(
        attn_out, "attn_out", 1,
        [attn_part, tok_rows, jnp.stack([out_b, gain_two, shift_two]), up_weight.astype(bf16),
         down_weight.astype(bf16)],
        [VM, VM, VM, ANY, ANY],
        [((2048, 2048), bf16), ((2048, 2048), bf16), ((4, 96, 2048), bf16), ((96, 2048), f32)],
        [ANY, ANY, ANY, VM],
        [pltpu.VMEM((2, 48, 2048), bf16), pltpu.VMEM((2, 96, 2048), bf16), pltpu.VMEM((96, 2048), bf16)]
        + sems(96, 8),
    )
    normed_two = normed_two.reshape(half, 2048)

    cot = lax.dynamic_slice_in_dim(cotangent, hi * half, half)
    hidden, gelu_back = jax.vjp(gelu_tanh, matmul(normed_two, up_w) + up_b)
    hidden = hidden.astype(bf16)
    mlp_part = matmul(hidden, down_w).astype(bf16).reshape(4, 96, 2048)
    down_part = contract_rows(hidden, cot).astype(bf16)
    grad_up = gelu_back(contract_cols(cot, down_w))[0].astype(bf16)
    up_bias_sum = jnp.sum(grad_up.astype(f32), axis=0)
    up_part = contract_rows(normed_two, grad_up).astype(bf16)
    norm_part = contract_cols(grad_up, up_w).astype(bf16).reshape(4, 96, 2048)
    out_rows, grad_middle, grad_attn, sums, up_grad, down_grad = kernel_call(
        mlp_back, "mlp_back", 2,
        [mlp_part, norm_part, middle, cot_rows, jnp.stack([down_b, gain_two]), up_part, down_part],
        [VM, VM, VM, VM, VM, ANY, ANY],
        [((96, 2048), bf16), ((96, 2048), f32), ((4, 96, 2048), bf16), ((8, 2048), f32),
         ((128, 1024), f32), ((1024, 128), f32)],
        [VM, VM, ANY, VM, VM, VM],
        [pltpu.VMEM((2, 48, 2048), bf16), pltpu.VMEM((2, 96, 2048), bf16)] * 2
        + [pltpu.VMEM((96, 2048), bf16)]
        + rs2d_bufs((128, 1024)) + rs2d_bufs((1024, 128)) + sems(128, 40),
    )
    grad_attn = grad_attn.reshape(half, 2048)

    out_part = contract_rows(attended, grad_attn).astype(bf16)
    grad_rows = heads_to_rows(contract_cols(grad_attn, out_w).astype(bf16), heads, half)
    probs_again = jnp.exp(
        jnp.where(allowed, contract_cols(query_rows, keys) * scale, NEG) - log_total
    )
    grad_probs = contract_cols(grad_rows, values)
    delta = jnp.sum(probs_again * grad_probs, axis=-1, keepdims=True)
    grad_scores = (probs_again * (grad_probs - delta)).astype(bf16)
    grad_query = rows_to_heads((matmul(grad_scores, keys) * scale).astype(bf16), heads, half)
    grad_keys = contract_rows(grad_scores, query_rows) * scale
    grad_values = contract_rows(probs_again.astype(bf16), grad_rows)
    pieces = jnp.concatenate([grad_keys, grad_values], 1).astype(bf16).reshape(5, half, 256)
    norm_part = contract_cols(grad_query, query_w).astype(bf16).reshape(4, 96, 2048)
    kv_grad, total = kernel_call(
        attn_back, "attn_back", 3,
        [pieces, norm_part], [VM, VM],
        [((4, 96, 256), bf16), ((96, 2048), f32)], [VM, VM],
        [pltpu.VMEM((2, 48, 2048), bf16), pltpu.VMEM((2, 96, 2048), bf16),
         pltpu.VMEM((4, half, 256), bf16), pltpu.VMEM((4, 96, 256), bf16),
         pltpu.VMEM((3, 96, 256), bf16)] + sems(24, 4),
    )
    kv_rows = lax.dynamic_index_in_dim(kv_grad, z, 0, keepdims=False)
    kv_grad = kv_grad.reshape(half, 256)
    query_bias_sum = jnp.sum(grad_query.astype(f32), axis=0)
    query_part = contract_rows(normed_one, grad_query).astype(bf16)
    keyval_part = contract_rows(normed_one, kv_grad).astype(bf16)
    value_bias_sum = jnp.sum(kv_grad[:, HD:].astype(f32), axis=0)
    grad_norm = total + contract_cols(kv_rows, keyval_w)
    center, inv = spread(tok_rows.astype(f32))
    norm = center * inv
    flow = grad_norm * gain_one
    in_rows = grad_middle + inv * (
        flow
        - jnp.mean(flow, axis=-1, keepdims=True)
        - norm * jnp.mean(flow * norm, axis=-1, keepdims=True)
    )
    gain_sum = jnp.sum(grad_norm * norm, axis=0)
    shift_sum = jnp.sum(grad_norm, axis=0)
    six = jnp.stack([gain_sum, shift_sum, sums[2], sums[0], sums[1], sums[3]])
    six = jnp.broadcast_to(six.reshape(6, 16, 128).transpose(1, 0, 2)[None], (2, 16, 6, 128))
    last = jnp.concatenate(
        [
            query_bias_sum.reshape(2, 2, 16, 8).transpose(0, 2, 1, 3).reshape(2, 16, 16),
            up_bias_sum.reshape(2, 8, 16, 8).transpose(0, 2, 1, 3).reshape(2, 16, 64),
            jnp.broadcast_to(value_bias_sum.reshape(16, 8)[None], (2, 16, 8)),
            jnp.zeros((2, 16, 40), f32),
        ],
        axis=-1,
    )
    small_part = jnp.concatenate([six, last[:, :, None], jnp.zeros((2, 16, 9, 128), f32)], 2)
    output, input_grad, query_grad, keyval_grad, out_grad, small_grad = kernel_call(
        finish, "finish", 4,
        [out_rows, in_rows.astype(bf16), query_part, keyval_part, out_part, small_part],
        [ANY] * 6,
        [((2, 4, 96, 2048), bf16), ((2, 4, 96, 2048), bf16), ((128, 256), f32), ((128, 256), f32),
         ((256, 128), f32), ((16, 128), f32)],
        [ANY, ANY, VM, VM, VM, VM],
        [pltpu.VMEM((16, 128), f32), pltpu.VMEM((3, 16, 128), f32), pltpu.VMEM((64, 256), f32)]
        + rs2d_bufs((128, 256)) + rs2d_bufs((64, 256)) + rs2d_bufs((256, 128))
        + rs2d_bufs((16, 128), f32) + sems(224, 72),
    )
    return (
        output.reshape(768, 2048),
        input_grad.reshape(768, 2048).astype(f32),
        small_grad[0],
        small_grad[1],
        query_grad,
        small_grad[6, :16].reshape(2, 8),
        keyval_grad,
        small_grad[6, 80:88],
        out_grad,
        small_grad[2],
        small_grad[3],
        small_grad[4],
        up_grad,
        small_grad[6, 16:80].reshape(8, 8),
        down_grad,
        small_grad[5],
    )


def solution(mesh):
    return jax.shard_map(
        body,
        mesh=mesh,
        in_specs=(
            P("dp", None), P("dp", None), P(), P("dp"), P("dp"), P("dp", "tensor"),
            P("tensor", "dp"), P("dp", None), P("dp"), P("tensor", "dp"), P("dp"), P("dp"),
            P("dp"), P("dp", "tensor"), P("tensor", "dp"), P("tensor", "dp"), P("dp"),
        ),
        out_specs=(
            P("dp", None), P("dp", None), P("dp"), P("dp"), P("dp", "tensor"),
            P("tensor", "dp"), P("dp", None), P("dp"), P("tensor", "dp"), P("dp"), P("dp"),
            P("dp"), P("dp", "tensor"), P("tensor", "dp"), P("tensor", "dp"), P("dp"),
        ),
        check_vma=False,
    )
```

time: 1080 us -> 453 us (0.42)
  waiting for transfers between devices: 561 us -> 0.01 us
  Pallas kernels: 0 us -> 266 us
  blocking collectives: 230 us -> 0 us
  other arithmetic: 99.1 us -> 44.4 us
  matrix products: 124 us -> 86 us
  between operations: 17.2 us -> 1.54 us
    psum x3 -> x0, waiting for transfers between devices: 352 us -> none  [the longest x1 154 us: body(): lax.psum(matmul(hidden, down_w).astype(jnp.bfloat16), 'tensor')]
    pallas_call x0 -> x5, Pallas kernels: none -> 266 us  [kernel_call(): pl.pallas_call(body, out_shape=[jax.ShapeDtypeStruct(s, d) for s, d in ou...]
    all_gather x8 -> x0, blocking collectives: 144 us -> none  [the longest x1 23.1 us: body(): lax.all_gather(query_bias.astype(bf16), 'dp', axis=1, tiled=True)]
    reduce_scatter x3 -> x0, waiting for transfers between devices: 127 us -> none  [the longest x1 66.8 us: body(): lax.psum_scatter(up_weight_grad.astype(jnp.bfloat16), 'dp', scatter_dimen...]
    unnamed x2 -> x0, blocking collectives: 86 us -> none
    all_gather x5 -> x0, waiting for transfers between devices: 66.3 us -> none  [the longest x1 37.9 us: body(): lax.all_gather(down_weight.astype(bf16), 'dp', axis=1, tiled=True)]
    convert_element_type x24 -> x4, other arithmetic: 35.8 us -> 10.4 us  [the longest x1 5.44 us: body(): input_grad.reshape(768, 2048).astype(f32)]
    reduce_sum x10 -> x6, other arithmetic: 25.9 us -> 5.46 us  [the longest x2 4.03 us: spread(): center = values - jnp.mean(values, axis=-1, keepdims=True)]
  transfers between devices with their start and end apart: 17 -> 2, of which waited for: 9 -> 0; matrix products, arithmetic and copies ran while one was open for 20% -> 5% of each run, Pallas kernels for 0% -> 0%
where the time goes in v1:
time: 453 us; the launch traced here: 447 us
  Pallas kernels  266 us (59%)
  matrix products  86 us (19%)
  other arithmetic  44.4 us (10%)
  local copies, waits for them, and re-layouts  43.4 us (10%)
  starting transfers between devices  5.88 us (1%)
    pallas_call x5, Pallas kernels, kernel_call(): pl.pallas_call(body, out_shape=[jax.ShapeDtypeStruct(s, d) for s, d in ou...  266 us
    dot_general x7, matrix products, contract_rows(): lax.dot_general(left, right, (((0,), (0,)), ((), ())), preferred_element_...  32.1 us
    dot_general x7, matrix products, contract_cols(): lax.dot_general(left, right, (((1,), (1,)), ((), ())), preferred_element_...  28.6 us
    dot_general x7, matrix products, matmul(): return jnp.dot(left, right, preferred_element_type=f32)  25.3 us
    unnamed x105, local copies, waits for them, and re-layouts  11.2 us
  transfers between devices with their start and end apart: 2, of which 0 were waited for; matrix products, arithmetic and copies ran while one was open for 5% of the time, Pallas kernels for 0%

profile of v1, /device:TPU:0, one launch (start us, length us, event | category | flops | bytes accessed | tf_op | source)
XLA Modules:
  0.0 446.9 jit_solution(3543653499676479058)
XLA Ops:
  10.5 33.6 %gather_first.1 = (bf16[2048,512]{1,0:T(8,128)(2,1)}, bf16[2048,256]{1,0:T(8,128)(2,1)}, bf16[512,2048]{1,0:T(8,128)(2,1)}, f32[2,16,16,128]{3,2,1,0:T(8,128)}) custom-call(bf16[128,256]{1,0:T(8,128)(2,1)} %convert_element_type.109.query_w, bf16[64,256]{1,0:T(8,128)(2,1)} %dynamic-slice_convert_fusion.keyval_w, ...), custom_call_target="tpu_custom_call" | custom-call | bytes 1048576 | tf_op jit(solution)/shard_map/gather_first/pallas_call | solution.py:307
  50.0 3.2 fusion.6
  55.0 2.4 collective-permute-start
  57.4 3.5 collective-permute-start.1
  62.4 3.1 fusion.25
  87.7 2.8 fusion.61
  92.2 2.6 copy-done.2
  94.8 2.5 convolution_convert_fusion.9
  98.2 3.9 convolution_convert_fusion.7
  102.1 62.9 %attn_out.1 = (bf16[2048,2048]{1,0:T(8,128)(2,1)}, bf16[2048,2048]{1,0:T(8,128)(2,1)}, bf16[4,96,2048]{2,1,0:T(8,128)(2,1)}, f32[96,2048]{1,0:T(8,128)}) custom-call(bf16[4,96,2048]{2,1,0:T(8,128)(2,1)} %bitcast.149, bf16[96,2048]{1,0:T(8,128)(2,1)} %copy-done.4, f32[3,2048]{1,0:T(4,128)} %pad_maximum_fusion.1.vecs, ...), custom_call_target="tpu_custom_call" | custom-call | bytes 1048576 | tf_op jit(solution)/shard_map/attn_out/pallas_call | solution.py:307
  165.0 6.4 %convolution_add_fusion = f32[384,2048]{1,0:T(8,128)S(1)} fusion(bf16[384,2048]{1,0:T(8,128)(2,1)} %bitcast.192, bf16[2048,2048]{1,0:T(8,128)(2,1)} %get-tuple-element.43, f32[2048]{0:T(1024)S(1)} %copy-done.31), kind=kOutput, calls=%fused_computation.34 | convolution fusion | flops 3222011904 | bytes 13115392 | tf_op jit(solution)/shard_map/dot_general | solution.py:616
  171.5 5.2 %convolution_convert_fusion.5 = bf16[384,2048]{1,0:T(8,128)(2,1)} fusion(bf16[2048,2048]{1,0:T(8,128)(2,1)S(1)} %copy-done.37, f32[384,2048]{1,0:T(8,128)S(1)} %convolution_add_fusion), kind=kOutput, calls=%fused_computation.36 | convolution fusion | flops 3229089792 | bytes 13107200 | tf_op jit(solution)/shard_map/dot_general | solution.py:616
  176.7 6.7 %convert_reduce_fusion.1 = (f32[2048]{0:T(1024)}, bf16[384,2048]{1,0:T(8,128)(2,1)S(1)}) fusion(f32[384,2048]{1,0:T(8,128)S(1)} %convolution_add_fusion, bf16[2048,2048]{1,0:T(8,128)(2,1)S(1)} %bitcast.189, bf16[768,2048]{1,0:T(8,128)(2,1)S(1)} %copy-done, s32[]{:T(128)S(6)} %select_n.44), kind=kOutput, calls=%fused_computation.27 | convolution fusion | flops 3241670656 | bytes 14688260 | tf_op jit(solution)/shard_map/dot_general | solution.py:624
  183.5 4.7 %convolution_convert_fusion.4 = bf16[384,2048]{1,0:T(8,128)(2,1)} fusion(bf16[384,2048]{1,0:T(8,128)(2,1)S(1)} %get-tuple-element.88, bf16[2048,2048]{1,0:T(8,128)(2,1)S(1)} %bitcast.187), kind=kOutput, calls=%fused_computation.35 | convolution fusion | flops 3222011904 | bytes 11534336 | tf_op jit(solution)/shard_map/dot_general | solution.py:624
  188.1 7.0 %convolution_convert_fusion.1.part_up = bf16[2048,2048]{1,0:T(8,128)(2,1)} fusion(bf16[384,2048]{1,0:T(8,128)(2,1)S(1)} %bitcast.193, bf16[384,2048]{1,0:T(8,128)(2,1)S(1)} %get-tuple-element.88), kind=kOutput, calls=%fused_computation.9 | convolution fusion | flops 3225419776 | bytes 11534336 | tf_op jit(solution)/shard_map/dot_general | solution.py:620
  195.1 7.3 %convolution_convert_fusion.part_down = bf16[2048,2048]{1,0:T(8,128)(2,1)} fusion(bf16[768,2048]{1,0:T(8,128)(2,1)S(1)} %copy-done, s32[]{:T(128)S(6)} %select_n.44, f32[384,2048]{1,0:T(8,128)S(1)} %copy-done.41), kind=kOutput, calls=%fused_computation.8 | convolution fusion | flops 3232497664 | bytes 13107204 | tf_op jit(solution)/shard_map/dot_general | solution.py:620
  202.4 65.1 %mlp_back.1 = (bf16[96,2048]{1,0:T(8,128)(2,1)}, f32[96,2048]{1,0:T(8,128)}, bf16[4,96,2048]{2,1,0:T(8,128)(2,1)}, f32[8,2048]{1,0:T(8,128)}, f32[128,1024]{1,0:T(8,128)}, /*index=5*/f32[1024,128]{1,0:T(8,128)}) custom-call(bf16[4,96,2048]{2,1,0:T(8,128)(2,1)} %bitcast.156, bf16[4,96,2048]{2,1,0:T(8,128)(2,1)} %bitcast.157, ...), custom_call_target="tpu_custom_call" | custom-call | bytes 1048576 | tf_op jit(solution)/shard_map/mlp_back/pallas_call | solution.py:307
  267.5 2.4 convolution_convert_fusion.11
  271.3 7.6 %multiply_reduce_fusion = (f32[1536]{0:T(1024)S(1)}, f32[1536,1920]{1,0:T(8,128)S(1)}) fusion(f32[1536,1920]{1,0:T(8,128)} %copy-done.2, f32[1536]{0:T(1024)S(1)} %log_add_fusion, bf16[1536,128]{0,1:T(8,128)(2,1)S(1)} %bitcast.164, bf16[1920,256]{1,0:T(8,128)(2,1)S(1)} %copy-done.7), kind=kOutput, calls=%fused_computation.1 | convolution fusion | flops 763820544 | bytes 24492032 | tf_op jit(solution)/shard_map/dot_general | solution.py:624
  279.1 5.9 %multiply_convert_fusion = (bf16[1536,1920]{1,0:T(8,128)(2,1)}, bf16[1920,1536]{0,1:T(8,128)(2,1)}) fusion(f32[1536,1920]{1,0:T(8,128)S(1)} %get-tuple-element.85, f32[1536,1920]{1,0:T(8,128)S(1)} %bitcast.148, f32[1536]{0:T(1024)S(1)} %get-tuple-element.84, f32[1536]{0:T(1024)S(1)} %log_add_fusion), kind=kLoop, calls=%fused_computation | loop fusion | flops 14745600 | bytes 35401728 | tf_op jit(solution)/shard_map/convert_element_type | solution.py:749
  285.0 5.3 %fusion.16 = bf16[1920,128]{1,0:T(8,128)(2,1)} fusion(bf16[1536,1920]{1,0:T(8,128)(2,1)} %get-tuple-element.66, bf16[1536,128]{1,0:T(8,128)(2,1)S(1)} %bitcast.155), kind=kOutput, calls=%fused_computation.42 | convolution fusion | flops 755466240 | bytes 6782976 | tf_op jit(solution)/shard_map/dot_general | solution.py:620
  290.3 2.5 fusion.17
  294.2 3.8 convolution_convert_fusion.6
  298.0 2.7 convolution_convert_fusion.3.part_query
  300.7 2.6 convolution_convert_fusion.2.part_out
  303.3 8.5 %copy.46 = bf16[1920,1536]{1,0:T(8,128)(2,1)} copy(bf16[1920,1536]{0,1:T(8,128)(2,1)} %get-tuple-element.67) | data formatting | bytes 11796480 | tf_op jit(solution)/shard_map/dot_general | solution.py:620
  311.8 4.4 convolution_convert_fusion.10
  317.4 29.0 %attn_back.1 = (bf16[4,96,256]{2,1,0:T(8,128)(2,1)}, f32[96,2048]{1,0:T(8,128)}) custom-call(bf16[5,384,256]{2,1,0:T(8,128)(2,1)} %pad_maximum_fusion.pieces, bf16[4,96,2048]{2,1,0:T(8,128)(2,1)} %bitcast.158), custom_call_target="tpu_custom_call" | custom-call | bytes 1048576 | tf_op jit(solution)/shard_map/attn_back/pallas_call | solution.py:307
  346.4 2.7 convolution_convert_fusion.8.part_keyval
  352.9 75.2 %finish.1 = (bf16[2,4,96,2048]{3,2,1,0:T(8,128)(2,1)}, bf16[2,4,96,2048]{3,2,1,0:T(8,128)(2,1)}, f32[128,256]{1,0:T(8,128)}, f32[128,256]{1,0:T(8,128)}, f32[256,128]{1,0:T(8,128)}, /*index=5*/f32[16,128]{1,0:T(8,128)}) custom-call(bf16[96,2048]{1,0:T(8,128)(2,1)} %get-tuple-element.46.out_rows, bf16[96,2048]{1,0:T(8,128)(2,1)} %fusion.40.in_rows, ...), custom_call_target="tpu_custom_call" | custom-call | bytes 1048576 | tf_op jit(solution)/shard_map/finish/pallas_call | solution.py:307
  432.3 5.4 %bitcast_convert_fusion = f32[768,2048]{1,0:T(8,128)} fusion(bf16[2,4,96,2048]{3,2,1,0:T(8,128)(2,1)} %get-tuple-element.53), kind=kLoop, calls=%fused_computation.26 | loop fusion | flops 1572864 | bytes 9437184 | tf_op jit(solution)/shard_map/convert_element_type | solution.py:805
  439.0 4.1 copy.67
  (193 shorter events, 60.5 us)
Async XLA Ops:
  0.6 76.9 %copy-start = (bf16[768,2048]{1,0:T(8,128)(2,1)S(1)}, bf16[768,2048]{1,0:T(8,128)(2,1)}, u32[]{:S(2)}) copy-start(bf16[768,2048]{1,0:T(8,128)(2,1)} %param.18) | copy-start | bytes 9437188
  8.9 40.0 %copy-start.3 = (bf16[768,2048]{1,0:T(8,128)(2,1)S(1)}, bf16[768,2048]{1,0:T(8,128)(2,1)}, u32[]{:S(2)}) copy-start(bf16[768,2048]{1,0:T(8,128)(2,1)} %param.17) | copy-start | bytes 9437188
  55.0 30.8 %collective-permute-start = (bf16[768,256]{1,0:T(8,128)(2,1)}, bf16[768,256]{1,0:T(8,128)(2,1)}, u32[]{:S(2)}, u32[]{:S(2)}) collective-permute-start(bf16[768,256]{1,0:T(8,128)(2,1)} %fusion.24), channel_id=1, source_target_pairs={{0,16},{8,24},{16,32},{24,40},{32,48},{40,56},{48,64},{56,72},{64,... | collective-permute-start | bytes 1179656 | tf_op jit(solution)/shard_map/ppermute | solution.py:634
  57.4 28.4 %collective-permute-start.1 = (bf16[768,256]{1,0:T(8,128)(2,1)}, bf16[768,256]{1,0:T(8,128)(2,1)}, u32[]{:S(2)}, u32[]{:S(2)}) collective-permute-start(bf16[768,256]{1,0:T(8,128)(2,1)} %fusion.24), channel_id=1, source_target_pairs={{0,8},{8,16},{16,24},{24,32},{32,40},{40,48},{48,56},{56,64},{64,7... | collective-permute-start | bytes 1179656 | tf_op jit(solution)/shard_map/ppermute | solution.py:634
  69.2 21.3 %copy-start.4 = (bf16[96,2048]{1,0:T(8,128)(2,1)}, bf16[96,2048]{1,0:T(8,128)(2,1)S(1)}, u32[]{:S(2)}) copy-start(bf16[96,2048]{1,0:T(8,128)(2,1)S(1)} %get-tuple-element.65.tok) | copy-start | bytes 1179652
  98.2 66.8 %copy-start.31 = (f32[2048]{0:T(1024)S(1)}, f32[2048]{0:T(1024)}, u32[]{:S(2)}) copy-start(f32[2048]{0:T(1024)} %add.157) | copy-start | bytes 24580
  165.0 6.5 %copy-start.37 = (bf16[2048,2048]{1,0:T(8,128)(2,1)S(1)}, bf16[2048,2048]{1,0:T(8,128)(2,1)}, u32[]{:S(2)}) copy-start(bf16[2048,2048]{1,0:T(8,128)(2,1)} %get-tuple-element.44) | copy-start | bytes 25165828
  165.0 11.7 %slice-start.5 = ((s8[8388608]{0:T(1024)(128)(4,1)}), s8[4194304]{0:T(1024)(128)(4,1)S(1)}, s32[]{:S(2)}) async-start(s8[8388608]{0:T(1024)(128)(4,1)} %bitcast.188), calls=%async_computation.5 | async-start | bytes 8388608
  171.5 5.2 %copy-start.40 = (f32[384,2048]{1,0:T(8,128)}, f32[384,2048]{1,0:T(8,128)S(1)}, u32[]{:S(2)}) copy-start(f32[384,2048]{1,0:T(8,128)S(1)} %convolution_add_fusion) | copy-start | bytes 9437188
  171.5 5.2 %slice-start.6 = ((s8[8388608]{0:T(1024)(128)(4,1)}), s8[4194304]{0:T(1024)(128)(4,1)S(1)}, s32[]{:S(2)}) async-start(s8[8388608]{0:T(1024)(128)(4,1)} %bitcast.188), calls=%async_computation.6 | async-start | bytes 8388608
  171.5 11.9 %slice-start.3 = ((s8[8388608]{0:T(1024)(128)(4,1)}), s8[4194304]{0:T(1024)(128)(4,1)S(1)}, s32[]{:S(2)}) async-start(s8[8388608]{0:T(1024)(128)(4,1)} %bitcast.186), calls=%async_computation.3 | async-start | bytes 8388608
  176.7 6.7 %slice-start.4 = ((s8[8388608]{0:T(1024)(128)(4,1)}), s8[4194304]{0:T(1024)(128)(4,1)S(1)}, s32[]{:S(2)}) async-start(s8[8388608]{0:T(1024)(128)(4,1)} %bitcast.186), calls=%async_computation.4 | async-start | bytes 8388608
  188.1 7.0 %copy-start.41 = (f32[384,2048]{1,0:T(8,128)S(1)}, f32[384,2048]{1,0:T(8,128)}, u32[]{:S(2)}) copy-start(f32[384,2048]{1,0:T(8,128)} %copy-done.40) | copy-start | bytes 9437188
  202.4 65.1 %copy-start.12 = (bf16[512,2048]{1,0:T(8,128)(2,1)S(1)}, bf16[512,2048]{1,0:T(8,128)(2,1)}, u32[]{:S(2)}) copy-start(bf16[512,2048]{1,0:T(8,128)(2,1)} %get-tuple-element.41) | copy-start | bytes 6291460
  271.3 7.6 %slice-start = ((s8[11796480]{0:T(1024)(128)(4,1)}), s8[4194304]{0:T(1024)(128)(4,1)S(1)}, s32[]{:S(2)}) async-start(s8[11796480]{0:T(1024)(128)(4,1)} %bitcast.147), calls=%async_computation | async-start | bytes 8388608
  271.3 7.6 %slice-start.1 = ((s8[11796480]{0:T(1024)(128)(4,1)}), s8[4194304]{0:T(1024)(128)(4,1)S(1)}, s32[]{:S(2)}) async-start(s8[11796480]{0:T(1024)(128)(4,1)} %bitcast.147), calls=%async_computation.1 | async-start | bytes 8388608
  271.3 7.8 %slice-start.2 = ((s8[11796480]{0:T(1024)(128)(4,1)}), s8[3407872]{0:T(1024)(128)(4,1)S(1)}, s32[]{:S(2)}) async-start(s8[11796480]{0:T(1024)(128)(4,1)} %bitcast.147), calls=%async_computation.2 | async-start | bytes 6815744
  279.1 5.9 %copy-start.14 = (bf16[48,4,8,128]{3,2,0,1:T(8,128)(2,1)S(1)}, bf16[48,4,8,128]{3,2,0,1:T(8,128)(2,1)}, u32[]{:S(2)}) copy-start(bf16[48,4,8,128]{3,2,0,1:T(8,128)(2,1)} %copy.60) | copy-start | bytes 1179652
  285.0 5.3 %copy-start.8 = (bf16[1536,1920]{1,0:T(8,128)(2,1)S(1)}, bf16[1536,1920]{1,0:T(8,128)(2,1)}, u32[]{:S(2)}) copy-start(bf16[1536,1920]{1,0:T(8,128)(2,1)} %get-tuple-element.66) | copy-start | bytes 17694724
  292.8 5.1 %copy-start.10 = (bf16[768,2048]{1,0:T(8,128)(2,1)S(1)}, bf16[768,2048]{1,0:T(8,128)(2,1)}, u32[]{:S(2)}) copy-start(bf16[768,2048]{1,0:T(8,128)(2,1)} %copy-done.9) | copy-start | bytes 9437188
  303.3 8.5 %copy-start.23 = (bf16[1536,128,1]{0,1,2:T(8,128)(2,1)S(1)}, bf16[1536,128,1]{0,1,2:T(8,128)(2,1)}, u32[]{:S(2)}) copy-start(bf16[1536,128,1]{0,1,2:T(8,128)(2,1)} %reshape.258) | copy-start | bytes 1179652
  316.2 30.1 %copy-start.11 = (bf16[768,2048]{1,0:T(8,128)(2,1)S(1)}, bf16[768,2048]{1,0:T(8,128)(2,1)}, u32[]{:S(2)}) copy-start(bf16[768,2048]{1,0:T(8,128)(2,1)} %copy-done.9) | copy-start | bytes 9437188
  317.3 32.0 %copy-start.29 = (f32[8,2048]{1,0:T(8,128)S(1)}, f32[8,2048]{1,0:T(8,128)}, u32[]{:S(2)}) copy-start(f32[8,2048]{1,0:T(8,128)} %get-tuple-element.51) | copy-start | bytes 196612
  317.3 32.1 %copy-start.5 = (bf16[96,2048]{1,0:T(8,128)(2,1)S(1)}, bf16[96,2048]{1,0:T(8,128)(2,1)}, u32[]{:S(2)}) copy-start(bf16[96,2048]{1,0:T(8,128)(2,1)} %copy-done.4) | copy-start | bytes 1179652
  317.3 32.1 %copy-start.17 = (bf16[2048,256]{1,0:T(8,128)(2,1)S(1)}, bf16[2048,256]{1,0:T(8,128)(2,1)}, u32[]{:S(2)}) copy-start(bf16[2048,256]{1,0:T(8,128)(2,1)} %get-tuple-element.40) | copy-start | bytes 3145732
  317.3 32.1 %copy-start.33 = (f32[96]{0:T(128)S(1)}, f32[96]{0:T(128)}, u32[]{:S(2)}) copy-start(f32[96]{0:T(128)} %copy-done.32) | copy-start | bytes 1156
  317.3 32.1 %copy-start.34 = (f32[96]{0:T(128)S(1)}, f32[96]{0:T(128)}, u32[]{:S(2)}) copy-start(f32[96]{0:T(128)} %add_rsqrt_fusion.1) | copy-start | bytes 1156
  439.0 7.7 %copy-start.1 = (bf16[768,2048]{1,0:T(8,128)(2,1)S(1)}, bf16[768,2048]{1,0:T(8,128)(2,1)}, u32[]{:S(2)}) copy-start(bf16[768,2048]{1,0:T(8,128)(2,1)} %param.18) | copy-start | bytes 9437188
  439.0 4.8 %copy-start.25 = (f32[128,256]{1,0:T(8,128)S(1)}, f32[128,256]{1,0:T(8,128)}, u32[]{:S(2)}) copy-start(f32[128,256]{1,0:T(8,128)} %get-tuple-element.117) | copy-start | bytes 393220
  439.0 5.5 %copy-start.24 = (f32[256,128]{1,0:T(8,128)S(1)}, f32[256,128]{1,0:T(8,128)}, u32[]{:S(2)}) copy-start(f32[256,128]{1,0:T(8,128)} %get-tuple-element.119) | copy-start | bytes 393220
  439.0 6.1 %copy-start.21 = (f32[128,1024]{1,0:T(8,128)S(1)}, f32[128,1024]{1,0:T(8,128)}, u32[]{:S(2)}) copy-start(f32[128,1024]{1,0:T(8,128)} %get-tuple-element.123) | copy-start | bytes 1572868
  439.0 6.9 %copy-start.20 = (f32[1024,128]{1,0:T(8,128)S(1)}, f32[1024,128]{1,0:T(8,128)}, u32[]{:S(2)}) copy-start(f32[1024,128]{1,0:T(8,128)} %get-tuple-element.125) | copy-start | bytes 1572868
  (19 other events, 63.1 us)
